TPU v7x, 32 devices: a whole 2x2x4 slice. The times are simulated.
32 devices in a mesh: wide: 8 (over z, x), narrow: 4 (over y, core).
Axes of the slice: x: 2, y: 2, z: 4, core: 2. Of those that a mesh axis runs over, the one named last changes fastest.
Arguments:
- hidden: bfloat16 [512, 4096], P('narrow', 'wide'), may hold values from -6 to 6
- attn_gain: float32 [4096], replicated, may hold values from 0.5 to 1.5
- query_weight: bfloat16 [4096, 4096], P(None, 'wide'), may hold values from -0.09375 to 0.09375
- key_weight: bfloat16 [4096, 1024], P('wide'), may hold values from -0.125 to 0.125
- value_weight: bfloat16 [4096, 1024], P('wide'), may hold values from -0.125 to 0.125
- out_weight: bfloat16 [4096, 4096], P('wide'), may hold values from -0.09375 to 0.09375
- cache_key: bfloat16 [8, 512, 128], replicated, may hold values from -600 to 600
- cache_value: bfloat16 [8, 512, 128], replicated, may hold values from -6 to 6
- mlp_gain: float32 [4096], replicated, may hold values from 0.5 to 1.5
- router_weight: bfloat16 [4096, 16], replicated, may hold values from -0.09375 to 0.09375
- expert_ids: int32 [512, 2], P('narrow'), may hold values from 0 to 15, all different within a row; in each aligned block of 16 rows (0 to 15, 16 to 31, ...) at most 4 rows name the same one
- gate_weight: bfloat16 [32, 4096, 3200], P('wide', None, 'narrow'), may hold values from -0.09375 to 0.09375
- up_weight: bfloat16 [32, 4096, 3200], P('wide', None, 'narrow'), may hold values from -0.09375 to 0.09375
- down_weight: bfloat16 [32, 3200, 4096], P('wide', 'narrow'), may hold values from -0.078125 to 0.078125
Outputs:
- layer_out: bfloat16 [512, 4096], P('narrow', 'wide')
Inputs may be any that keep to these rules, and one draw needn't show every extreme that they name: `expert_ids`: in each aligned block of 16 rows no expert is named by more than 4 rows, and in every block some expert by exactly 4; the two experts of a row differ.
All inputs are finite; a program needn't handle non-finite values.
Results may differ from a plain program's by a relative error of at most 0.012.
The roundings to bfloat16 on the way count: a program that leaves them out, or rounds other values in their place, can miss the bound.
Values may be sent and summed in bfloat16 or wider, within the bound.
No kernel may reach another device: no remote copies, remote signals or barrier semaphores. Data moves between devices by JAX's collectives and lax.ppermute only.
A program may use at most 192 MiB of HBM per device.

v0:
```python
import jax
import jax.numpy as jnp
from jax import lax
from jax.sharding import PartitionSpec as P

SPLIT = 2
CAPD = 4
epsilon = 1e-05


def layer_normed(values, gain):
    average = jnp.mean(values, axis=-1, keepdims=True)
    centered = values - average
    variance = jnp.mean(centered * centered, axis=-1, keepdims=True)
    return centered * lax.rsqrt(variance + epsilon) * gain


def slot_targets(routing, experts, capacity):
    blocks = routing.shape[0]
    flat_ids = routing.reshape(blocks, -1)
    onehot = (flat_ids[:, :, None] == jnp.arange(experts, dtype=jnp.int32)[None, None, :]).astype(
        jnp.int32
    )
    earlier = jnp.cumsum(onehot, axis=1) - onehot
    position = jnp.sum(earlier * onehot, axis=2)
    return (flat_ids * capacity + position).reshape(routing.shape)


def fill_buffer(normed, target, slot_count):
    matches = (target[:, :, :, None] == jnp.arange(slot_count, dtype=jnp.int32)).astype(
        jnp.bfloat16
    )
    placing = jnp.sum(matches, axis=2)
    return jnp.einsum("btj,btd->bjd", placing, normed, preferred_element_type=jnp.float32).astype(
        jnp.bfloat16
    )


def pair_weights(logits, routing):
    picked = jnp.take_along_axis(logits, routing, axis=-1)
    leading = jax.nn.sigmoid(picked[..., 0] - picked[..., 1])
    return jnp.stack([leading, 1.0 - leading], axis=-1)


def gather_back(results, target, weights):
    blocks, slot_count = (results.shape[0], results.shape[1])
    flat_rows = results.reshape(blocks * slot_count, results.shape[2])
    row_index = target + (jnp.arange(blocks, dtype=jnp.int32) * slot_count)[:, None, None]
    picked = jnp.take(flat_rows, row_index.reshape(-1), axis=0).reshape(
        target.shape + (results.shape[2],)
    )
    return jnp.sum(picked * weights[..., None], axis=2)


def expert_terms(arrived, w_gate, w_up, w_down):
    gate_term = jnp.einsum("gscd,sdf->gscf", arrived, w_gate, preferred_element_type=jnp.float32)
    up_term = jnp.einsum("gscd,sdf->gscf", arrived, w_up, preferred_element_type=jnp.float32)
    active = (jax.nn.silu(gate_term) * up_term).astype(jnp.bfloat16)
    return jnp.einsum("gscf,sfd->gscd", active, w_down, preferred_element_type=jnp.float32)


def attend(queries, all_keys, all_values, first_row, context):
    row_count, heads_here, head_size = queries.shape
    kv_here = all_keys.shape[0]
    grouped = queries.reshape(row_count, kv_here, heads_here // kv_here, head_size)
    scale_factor = head_size ** (-0.5)
    scores = (
        jnp.einsum("rgqd,gkd->gqrk", grouped, all_keys, preferred_element_type=jnp.float32)
        * scale_factor
    )
    row_ids = first_row + jnp.arange(row_count, dtype=jnp.int32)
    key_ids = jnp.arange(all_keys.shape[1], dtype=jnp.int32) - context
    allowed = key_ids[None, :] <= row_ids[:, None]
    scores = jnp.where(allowed[None, None], scores, -1e30)
    highest = jnp.max(scores, axis=3, keepdims=True)
    weights = jnp.exp(scores - highest)
    weights = (weights / jnp.sum(weights, axis=3, keepdims=True)).astype(jnp.bfloat16)
    mixed = jnp.einsum(
        "gqrk,gkd->rgqd", weights, all_values, preferred_element_type=jnp.float32
    ).astype(jnp.bfloat16)
    return mixed.reshape(row_count, heads_here, head_size)


def body(
    hidden,
    attn_gain,
    query_weight,
    key_weight,
    value_weight,
    out_weight,
    cache_key,
    cache_value,
    mlp_gain,
    router_weight,
    expert_ids,
    gate_weight,
    up_weight,
    down_weight,
):
    wide_count = lax.axis_size("wide")
    wide_index = lax.axis_index("wide")
    narrow_index = lax.axis_index("narrow")
    full_rows = lax.all_gather(hidden, "wide", axis=1, tiled=True)
    row_count, feature_count = full_rows.shape
    kv_total, context, head_size = cache_key.shape
    heads_here = query_weight.shape[1] // head_size
    share = heads_here * wide_count // kv_total
    kv_here = max(heads_here // share, 1)
    kv_start = wide_index * heads_here // share
    normed = layer_normed(full_rows.astype(jnp.float32), attn_gain).astype(jnp.bfloat16)
    queries = jnp.dot(normed, query_weight, preferred_element_type=jnp.float32).astype(jnp.bfloat16)
    feature_share = key_weight.shape[0]
    normed_part = lax.dynamic_slice_in_dim(normed, wide_index * feature_share, feature_share, 1)
    key_term = jnp.dot(normed_part, key_weight, preferred_element_type=jnp.float32)
    value_term = jnp.dot(normed_part, value_weight, preferred_element_type=jnp.float32)
    key_cols, value_cols = lax.psum((key_term, value_term), "wide")
    key_cols = key_cols.astype(jnp.bfloat16)
    value_cols = value_cols.astype(jnp.bfloat16)
    fresh_keys = lax.dynamic_slice_in_dim(key_cols, kv_start * head_size, kv_here * head_size, 1)
    fresh_values = lax.dynamic_slice_in_dim(
        value_cols, kv_start * head_size, kv_here * head_size, 1
    )
    span_key_rows, span_value_rows = (
        lax.all_gather(fresh_keys, "narrow", axis=0, tiled=True),
        lax.all_gather(fresh_values, "narrow", axis=0, tiled=True),
    )
    own_cache_key = lax.dynamic_slice_in_dim(cache_key, kv_start, kv_here, 0)
    own_cache_value = lax.dynamic_slice_in_dim(cache_value, kv_start, kv_here, 0)
    all_keys = jnp.concatenate(
        [own_cache_key, span_key_rows.reshape(-1, kv_here, head_size).transpose(1, 0, 2)], axis=1
    )
    all_values = jnp.concatenate(
        [own_cache_value, span_value_rows.reshape(-1, kv_here, head_size).transpose(1, 0, 2)],
        axis=1,
    )
    attended = attend(
        queries.reshape(row_count, heads_here, head_size),
        all_keys,
        all_values,
        narrow_index * row_count,
        context,
    )
    attended = attended.reshape(row_count, heads_here * head_size)
    experts = router_weight.shape[1]
    capacity = CAPD
    slot_count = experts * SPLIT
    slots_here = gate_weight.shape[0]
    block_rows = row_count // wide_count
    head_mix = lax.psum_scatter(
        jnp.dot(attended, out_weight, preferred_element_type=jnp.float32),
        "wide",
        scatter_dimension=0,
        tiled=True,
    )
    own_rows = lax.dynamic_slice_in_dim(full_rows, wide_index * block_rows, block_rows, 0)
    residual = (own_rows.astype(jnp.float32) + head_mix).astype(jnp.bfloat16)
    normed_two = layer_normed(residual.astype(jnp.float32), mlp_gain).astype(jnp.bfloat16)
    logits = jnp.dot(normed_two, router_weight, preferred_element_type=jnp.float32)[None]
    routing = lax.dynamic_slice_in_dim(expert_ids, wide_index * block_rows, block_rows, 0)[None]
    target = slot_targets(routing, experts, capacity)
    buffer = fill_buffer(normed_two[None], target, experts * capacity)
    buffer = jnp.broadcast_to(
        buffer.reshape(experts, 1, capacity, feature_count),
        (experts, SPLIT, capacity, feature_count),
    )
    arrived = lax.all_to_all(
        buffer.reshape(slot_count, capacity, feature_count),
        "wide",
        split_axis=0,
        concat_axis=0,
        tiled=True,
    )
    arrived = arrived.reshape(wide_count, slots_here, capacity, feature_count)
    partial_out = expert_terms(
        lax.all_gather(arrived, "narrow", axis=0, tiled=True), gate_weight, up_weight, down_weight
    )
    reduced = lax.psum_scatter(partial_out, "narrow", scatter_dimension=0, tiled=True).astype(
        jnp.bfloat16
    )
    returned = lax.all_to_all(reduced, "wide", split_axis=0, concat_axis=1, tiled=True)
    summed = jnp.sum(
        returned.reshape(1, experts, SPLIT, capacity, feature_count).astype(jnp.float32), axis=2
    )
    mixture = gather_back(
        summed.reshape(1, experts * capacity, feature_count), target, pair_weights(logits, routing)
    )
    result = (residual.astype(jnp.float32) + mixture[0]).astype(jnp.bfloat16)
    final_out = lax.all_to_all(result, "wide", split_axis=1, concat_axis=0, tiled=True)
    return final_out


def solution(mesh):
    placed = (
        P("narrow", "wide"),
        P(),
        P(None, "wide"),
        P("wide", None),
        P("wide", None),
        P("wide", None),
        P(),
        P(),
        P(),
        P(),
        P("narrow", None),
        P("wide", None, "narrow"),
        P("wide", None, "narrow"),
        P("wide", "narrow", None),
    )
    return jax.shard_map(
        body, mesh=mesh, in_specs=placed, out_specs=P("narrow", "wide"), check_vma=False
    )
```

profile of v0, /device:TPU:0, one launch (start us, length us, event | category | flops | bytes accessed | tf_op | source)
XLA Modules:
  0.0 455.7 jit_solution(893464131646840608)
XLA Ops:
  6.5 0.7 all-gather.3.cloned.1.call-update
  7.4 0.9 constant_dynamic-slice_fusion.1
  8.3 0.9 constant_dynamic-slice_fusion.2
  9.2 0.2 broadcast_compare_fusion
  9.4 42.1 %all-gather.3.cloned.1.call-done = bf16[128,4096]{1,0:T(8,128)(2,1)} async-done(((bf16[128,512]{1,0:T(8,128)(2,1)}), bf16[128,4096]{1,0:T(8,128)(2,1)}) %all-gather.3.cloned.1.call-update) | async-done | bytes 1048592 | tf_op jit(solution)/shard_map/all_gather | solution.py:103
  51.5 1.5 convert_reduce_fusion
  53.1 1.7 fusion.11
  54.8 0.4 fusion.13
  55.2 3.0 fusion.21
  58.2 0.3 fusion.35
  58.5 0.9 copy-done.4
  59.4 0.3 fusion.37
  59.7 71.9 %all-reduce.2 = (bf16[128,1024]{1,0:T(8,128)(2,1)S(1)}, bf16[128,1024]{1,0:T(8,128)(2,1)S(1)}) all-reduce(f32[128,1024]{1,0:T(8,128)S(1)} %fusion.35, f32[128,1024]{1,0:T(8,128)S(1)} %fusion.37), channel_id=1, replica_groups=mesh['wide'=8,'narrow'=4] {'wide'}, use_global_device_ids=true, to_apply=%region_3.4 | all-reduce | flops 262144 | bytes 1572864 | tf_op jit(solution)/shard_map/psum | solution.py:116
  131.6 5.4 %all_gather.14 = bf16[512,128]{1,0:T(8,128)(2,1)S(1)} all-gather(bf16[128,128]{1,0:T(8,128)(2,1)S(1)} %dynamic-slice_convert_fusion), channel_id=1, replica_groups=mesh['wide'=8,'narrow'=4] {'narrow'}, dimensions={0}, use_global_device_ids=true | all-gather | bytes 163840 | tf_op jit(solution)/shard_map/all_gather | solution.py:124
  137.0 5.4 %all_gather.13 = bf16[512,128]{1,0:T(8,128)(2,1)S(1)} all-gather(bf16[128,128]{1,0:T(8,128)(2,1)S(1)} %dynamic-slice_convert_fusion.1), channel_id=1, replica_groups=mesh['wide'=8,'narrow'=4] {'narrow'}, dimensions={0}, use_global_device_ids=true | all-gather | bytes 163840 | tf_op jit(solution)/shard_map/all_gather | solution.py:125
  142.5 0.4 fusion.53
  142.9 0.3 fusion.14
  143.2 0.5 convolution_convert_fusion.2
  143.8 1.6 copy-done.3
  145.4 2.1 fusion.54
  147.6 0.6 copy-done.7
  149.0 67.0 %reduce-scatter.3.cloned.1.call-done = f32[16,4096]{1,0:T(8,128)} async-done(((f32[128,4096]{1,0:T(8,128)}), f32[16,4096]{1,0:T(8,128)}) %reduce-scatter.3.cloned.1.call-update) | async-done | bytes 262160 | tf_op jit(solution)/shard_map/reduce_scatter | solution.py:149
  216.0 1.1 convert_reduce_fusion.2
  217.1 0.2 fusion.25
  217.3 0.3 convolution_convert_fusion
  217.7 0.2 broadcast_in_dim.37
  217.9 0.5 broadcast_in_dim.58
  218.3 27.7 %all_to_all.33 = bf16[32,4,4096]{2,1,0:T(4,128)(2,1)S(1)} all-to-all(bf16[32,4,4096]{2,1,0:T(4,128)(2,1)S(1)} %bitcast.107), channel_id=1, replica_groups=mesh['wide'=8,'narrow'=4] {'wide'}, dimensions={0} | all-to-all | bytes 2097152 | tf_op jit(solution)/shard_map/all_to_all | solution.py:166
  246.0 1.6 copy.64
  247.6 0.2 reduce-scatter.5.cloned.1.call-start
  247.8 33.3 %all-gather.5.cloned.1.call-done = bf16[32,4,4,4096]{3,0,2,1:T(8,128)(2,1)} async-done(((bf16[8,4,4,4096]{3,0,2,1:T(8,128)(2,1)}), bf16[32,4,4,4096]{3,0,2,1:T(8,128)(2,1)}) %all-gather.5.cloned.1.call-update) | async-done | bytes 4194320 | tf_op jit(solution)/shard_map/all_gather | solution.py:175
  281.1 16.0 %fusion.4 = f32[4,32,4,800]{3,1,2,0:T(8,128)} fusion(bf16[32,4,4,4096]{3,0,2,1:T(8,128)(2,1)} %all-gather.5.cloned.1.call-done, bf16[4,4096,800]{1,2,0:T(8,128)(2,1)} %param.25), kind=kOutput, calls=%fused_computation.6 | convolution fusion | flops 3355443200 | bytes 32047104 | tf_op jit(solution)/shard_map/gscd,sdf->gscf/dot_general | solution.py:56
  297.2 15.3 %fusion.15 = bf16[32,4,4,800]{3,0,2,1:T(8,128)(2,1)S(1)} fusion(f32[4,32,4,800]{3,1,2,0:T(8,128)} %fusion.4, bf16[32,4,4,4096]{3,0,2,1:T(8,128)(2,1)} %all-gather.5.cloned.1.call-done, bf16[4,4096,800]{1,2,0:T(8,128)(2,1)} %param.26), kind=kOutput, calls=%fused_computation.23 | convolution fusion | flops 3357900800 | bytes 32866304 | tf_op jit(solution)/shard_map/gscd,sdf->gscf/dot_general | solution.py:57
  312.5 16.2 %fusion.6 = f32[32,4,4,4096]{3,0,2,1:T(8,128)} fusion(bf16[32,4,4,800]{3,0,2,1:T(8,128)(2,1)S(1)} %fusion.15, bf16[4,800,4096]{2,1,0:T(8,128)(2,1)} %param.27), kind=kOutput, calls=%fused_computation.8 | convolution fusion | flops 3355443200 | bytes 35422208 | tf_op jit(solution)/shard_map/gscf,sfd->gscd/dot_general | solution.py:59
  328.7 71.5 %reduce-scatter.5.cloned.1.call-done = f32[8,4,4,4096]{3,0,2,1:T(8,128)} async-done(((f32[32,4,4,4096]{3,0,2,1:T(8,128)}), f32[8,4,4,4096]{3,0,2,1:T(8,128)}) %reduce-scatter.5.cloned.1.call-update) | async-done | bytes 2097168 | tf_op jit(solution)/shard_map/reduce_scatter | solution.py:177
  400.2 1.7 convert_element_type.112
  402.0 1.8 copy.65
  403.8 5.5 %all-to-all-start.1 = ((bf16[8,4,4,4096]{3,2,1,0:T(4,128)(2,1)}), bf16[8,4,4,4096]{3,2,1,0:T(4,128)(2,1)S(1)}, u32[]{:S(2)}, u32[]{:S(2)}) async-start(bf16[8,4,4,4096]{3,2,1,0:T(4,128)(2,1)} %copy.65), calls=%async_computation.3 | async-start | bytes 2097152 | tf_op jit(solution)/shard_map/all_to_all | solution.py:180
  409.8 0.2 fusion.49
  410.0 0.7 gather_fusion.1
  411.0 23.9 %all-to-all-done.1 = bf16[8,4,4,4096]{3,2,1,0:T(4,128)(2,1)S(1)} async-done(((bf16[8,4,4,4096]{3,2,1,0:T(4,128)(2,1)}), bf16[8,4,4,4096]{3,2,1,0:T(4,128)(2,1)S(1)}, u32[]{:S(2)}, u32[]{:S(2)}) %all-to-all-start.1) | async-done | bytes 1048608 | tf_op jit(solution)/shard_map/all_to_all | solution.py:180
  434.9 0.6 convert_reduce_fusion.1
  435.6 0.4 reshape_reshape.9
  435.9 0.7 gather_fusion
  436.7 0.3 gather.13
  437.0 0.8 multiply_reduce_fusion
  437.8 10.7 %all_to_all.34 = bf16[16,8,512]{2,0,1:T(8,128)(2,1)S(1)} all-to-all(bf16[16,8,512]{2,0,1:T(8,128)(2,1)S(1)} %bitcast.109), channel_id=1, replica_groups=mesh['wide'=8,'narrow'=4] {'wide'}, dimensions={1} | all-to-all | bytes 262144 | tf_op jit(solution)/shard_map/all_to_all | solution.py:188
  448.5 0.7 copy.92
  (55 shorter events, 1.8 us)
Async XLA Ops:
  6.5 51.6 %copy-start = (bf16[512,1024]{1,0:T(8,128)(2,1)S(1)}, bf16[512,1024]{1,0:T(8,128)(2,1)}, u32[]{:S(2)}) copy-start(bf16[512,1024]{1,0:T(8,128)(2,1)} %param.17) | copy-start | bytes 3145732
  6.5 48.2 %copy-start.5 = (f32[4096]{0:T(1024)S(1)}, f32[4096]{0:T(1024)}, u32[]{:S(2)}) copy-start(f32[4096]{0:T(1024)} %param.15) | copy-start | bytes 49156
  6.5 45.0 %all-gather.3.cloned.1.call-start = ((), (), s32[]{:S(2)}) async-start(), calls=%async_computation.5 | async-start | bytes 1179648 | tf_op jit(solution)/shard_map/all_gather | solution.py:103
  7.3 208.7 %reduce-scatter.3.cloned.1.call-start = ((), (), s32[]{:S(2)}) async-start(), calls=%async_computation.6 | async-start | bytes 2359296 | tf_op jit(solution)/shard_map/reduce_scatter | solution.py:149
  51.5 3.2 copy-start.2
  58.1 1.2 copy-start.4
  143.2 2.2 copy-start.3
  147.5 0.7 copy-start.7
  147.5 69.8 %copy-start.6 = (f32[4096]{0:T(1024)S(1)}, f32[4096]{0:T(1024)}, u32[]{:S(2)}) copy-start(f32[4096]{0:T(1024)} %param.22) | copy-start | bytes 49156
  147.5 133.6 %all-gather.5.cloned.1.call-start = ((), (), s32[]{:S(2)}) async-start(), calls=%async_computation.7 | async-start | bytes 5242880 | tf_op jit(solution)/shard_map/all_gather | solution.py:175
  247.6 152.6 %reduce-scatter.5.cloned.1.call-start = ((), (), s32[]{:S(2)}) async-start(), calls=%async_computation.8 | async-start | bytes 10485760 | tf_op jit(solution)/shard_map/reduce_scatter | solution.py:177
  402.0 7.8 %copy-start.8 = (bf16[4096,16]{0,1:T(8,128)(2,1)S(1)}, bf16[4096,16]{0,1:T(8,128)(2,1)}, u32[]{:S(2)}) copy-start(bf16[4096,16]{0,1:T(8,128)(2,1)} %param.23) | copy-start | bytes 393220
  403.8 31.2 %all-to-all-start.1 = ((bf16[8,4,4,4096]{3,2,1,0:T(4,128)(2,1)}), bf16[8,4,4,4096]{3,2,1,0:T(4,128)(2,1)S(1)}, u32[]{:S(2)}, u32[]{:S(2)}) async-start(bf16[8,4,4,4096]{3,2,1,0:T(4,128)(2,1)} %copy.65), calls=%async_computation.3 | async-start | bytes 2097152 | tf_op jit(solution)/shard_map/all_to_all | solution.py:180
  435.9 13.3 %copy-start.1 = (bf16[512,1024]{1,0:T(8,128)(2,1)S(1)}, bf16[512,1024]{1,0:T(8,128)(2,1)}, u32[]{:S(2)}) copy-start(bf16[512,1024]{1,0:T(8,128)(2,1)} %param.17) | copy-start | bytes 3145732
Sparse Core Ops, SparseCore 0:
  9.4 42.1 all-gather.2
  147.6 68.2 reduce-scatter.2
  247.7 33.3 all-gather.4
  328.8 71.3 reduce-scatter.4
where the time goes:
time: 456 us
  waiting for transfers between devices  239 us (52%)
  blocking collectives  121 us (27%)
  matrix products  54.8 us (12%)
  between operations  13.5 us (3%)
  local copies, waits for them, and re-layouts  12.9 us (3%)
  other arithmetic  9.11 us (2%)
  starting transfers between devices  5.82 us (1%)
    psum x1, blocking collectives, body(): key_cols, value_cols = lax.psum((key_term, value_term), 'wide')  71.9 us
    reduce_scatter x1, waiting for transfers between devices, body(): lax.psum_scatter(partial_out, 'narrow', scatter_dimension=0, tiled=True)  71.5 us
    reduce_scatter x1, waiting for transfers between devices, body(): lax.psum_scatter(jnp.dot(attended, out_weight, preferred_element_type=jnp...  67 us
    all_gather x1, waiting for transfers between devices, body(): full_rows = lax.all_gather(hidden, 'wide', axis=1, tiled=True)  42.1 us
    all_gather x1, waiting for transfers between devices, body(): lax.all_gather(arrived, 'narrow', axis=0, tiled=True)  33.3 us
    all_to_all x1, blocking collectives, body(): lax.all_to_all(buffer.reshape(slot_count, capacity, feature_count), 'wide...  27.7 us
    all_to_all x1, waiting for transfers between devices, body(): lax.all_to_all(reduced, 'wide', split_axis=0, concat_axis=1, tiled=True)  23.9 us
    dot_general x1, matrix products, expert_terms(): jnp.einsum('gscf,sfd->gscd', active, w_down, preferred_element_type=jnp.f...  16.2 us
  transfers between devices with their start and end apart: 5, of which 5 were waited for; matrix products, arithmetic and copies ran while one was open for 1% of the time, Pallas kernels for 0%

commit v1 on v0

--- a/solution.py
+++ b/solution.py
@@ -6,6 +6,17 @@
 SPLIT = 2
 CAPD = 4
 epsilon = 1e-05
+
+
+def split_up(x, dim, devices):
+    before, after = (x.shape[:dim], x.shape[dim + 1 :])
+    return jnp.moveaxis(x.reshape(*before, devices, -1, *after), dim, 0)
+
+
+def laid_out(blocks, dim):
+    blocks = jnp.moveaxis(blocks, 0, dim)
+    lengths = blocks.shape
+    return blocks.reshape(*lengths[:dim], lengths[dim] * lengths[dim + 1], *lengths[dim + 2 :])
 
 
 def layer_normed(values, gain):
@@ -163,13 +174,15 @@
         buffer.reshape(experts, 1, capacity, feature_count),
         (experts, SPLIT, capacity, feature_count),
     )
-    arrived = lax.all_to_all(
-        buffer.reshape(slot_count, capacity, feature_count),
-        "wide",
-        split_axis=0,
-        concat_axis=0,
-        tiled=True,
-    )
+    shard = buffer.reshape(slot_count, capacity, feature_count)
+    size, index = (lax.axis_size("wide"), lax.axis_index("wide"))
+    parts = split_up(shard, 0, size)
+    finished = [parts[index]]
+    for lap in range(1, size):
+        sent = parts[index ^ lap]
+        finished.append(lax.ppermute(sent, "wide", [(i, i ^ lap) for i in range(size)]))
+    parts = jnp.stack(finished)[index ^ jnp.arange(size)]
+    arrived = laid_out(parts, 0)
     arrived = arrived.reshape(wide_count, slots_here, capacity, feature_count)
     partial_out = expert_terms(
         lax.all_gather(arrived, "narrow", axis=0, tiled=True), gate_weight, up_weight, down_weight

time: 456 us -> 458 us (level)
  blocking collectives: 121 us -> 93.4 us
  waiting for transfers between devices: 239 us -> 254 us
  starting transfers between devices: 5.82 us -> 17.3 us
    all_to_all x1 -> x0, blocking collectives: 27.7 us -> none  [body(): lax.all_to_all(buffer.reshape(slot_count, capacity, feature_count), 'wide...]
    ppermute x0 -> x7, waiting for transfers between devices: none -> 12.2 us  [body(): lax.ppermute(sent, 'wide', [(i, i ^ lap) for i in range(size)])]
    ppermute x0 -> x7, starting transfers between devices: none -> 11.4 us  [body(): lax.ppermute(sent, 'wide', [(i, i ^ lap) for i in range(size)])]
  transfers between devices with their start and end apart: 5 -> 12, of which waited for: 5 -> 8; matrix products, arithmetic and copies ran while one was open for 1% -> 1% of each run, Pallas kernels for 0% -> 0%
where the time goes in v1:
time: 458 us; the launch traced here: 457 us
  waiting for transfers between devices  254 us (55%)
  blocking collectives  93.4 us (20%)
  matrix products  54.8 us (12%)
  starting transfers between devices  17.3 us (4%)
  local copies, waits for them, and re-layouts  15.3 us (3%)
  between operations  13.6 us (3%)
  other arithmetic  9.13 us (2%)
    psum x1, blocking collectives, body(): key_cols, value_cols = lax.psum((key_term, value_term), 'wide')  71.9 us
    reduce_scatter x1, waiting for transfers between devices, body(): lax.psum_scatter(partial_out, 'narrow', scatter_dimension=0, tiled=True)  71.5 us
    reduce_scatter x1, waiting for transfers between devices, body(): lax.psum_scatter(jnp.dot(attended, out_weight, preferred_element_type=jnp...  67 us
    all_gather x1, waiting for transfers between devices, body(): full_rows = lax.all_gather(hidden, 'wide', axis=1, tiled=True)  42.1 us
    all_gather x1, waiting for transfers between devices, body(): lax.all_gather(arrived, 'narrow', axis=0, tiled=True)  36.3 us
    all_to_all x1, waiting for transfers between devices, body(): lax.all_to_all(reduced, 'wide', split_axis=0, concat_axis=1, tiled=True)  23.9 us
    dot_general x1, matrix products, expert_terms(): jnp.einsum('gscf,sfd->gscd', active, w_down, preferred_element_type=jnp.f...  16.2 us
    dot_general x1, matrix products, expert_terms(): jnp.einsum('gscd,sdf->gscf', arrived, w_gate, preferred_element_type=jnp....  16.1 us
  transfers between devices with their start and end apart: 12, of which 8 were waited for; matrix products, arithmetic and copies ran while one was open for 1% of the time, Pallas kernels for 0%

profile of v1, /device:TPU:0, one launch (start us, length us, event | category | flops | bytes accessed | tf_op | source)
XLA Modules:
  0.0 457.1 jit_solution(263289804408212877)
XLA Ops:
  6.5 0.7 all-gather.4.cloned.1.call-update
  7.4 0.9 constant_dynamic-slice_fusion.1
  8.3 0.9 constant_dynamic-slice_fusion.2
  9.4 42.1 %all-gather.4.cloned.1.call-done = bf16[128,4096]{1,0:T(8,128)(2,1)} async-done(((bf16[128,512]{1,0:T(8,128)(2,1)}), bf16[128,4096]{1,0:T(8,128)(2,1)}) %all-gather.4.cloned.1.call-update) | async-done | bytes 1048592 | tf_op jit(solution)/shard_map/all_gather | solution.py:114
  51.5 1.5 convert_reduce_fusion
  53.1 1.7 fusion.11
  54.8 0.4 fusion.13
  55.2 3.0 fusion.21
  58.5 0.9 copy-done.4
  59.7 71.9 %all-reduce.2 = (bf16[128,1024]{1,0:T(8,128)(2,1)S(1)}, bf16[128,1024]{1,0:T(8,128)(2,1)S(1)}) all-reduce(f32[128,1024]{1,0:T(8,128)S(1)} %fusion.35, f32[128,1024]{1,0:T(8,128)S(1)} %fusion.37), channel_id=1, replica_groups=mesh['wide'=8,'narrow'=4] {'wide'}, use_global_device_ids=true, to_apply=%region_3.4 | all-reduce | flops 262144 | bytes 1572864 | tf_op jit(solution)/shard_map/psum | solution.py:127
  131.6 5.4 %all_gather.14 = bf16[512,128]{1,0:T(8,128)(2,1)S(1)} all-gather(bf16[128,128]{1,0:T(8,128)(2,1)S(1)} %dynamic-slice_convert_fusion), channel_id=1, replica_groups=mesh['wide'=8,'narrow'=4] {'narrow'}, dimensions={0}, use_global_device_ids=true | all-gather | bytes 163840 | tf_op jit(solution)/shard_map/all_gather | solution.py:135
  137.0 5.4 %all_gather.13 = bf16[512,128]{1,0:T(8,128)(2,1)S(1)} all-gather(bf16[128,128]{1,0:T(8,128)(2,1)S(1)} %dynamic-slice_convert_fusion.1), channel_id=1, replica_groups=mesh['wide'=8,'narrow'=4] {'narrow'}, dimensions={0}, use_global_device_ids=true | all-gather | bytes 163840 | tf_op jit(solution)/shard_map/all_gather | solution.py:136
  142.5 0.4 fusion.54
  143.2 0.5 convolution_convert_fusion.2
  143.8 1.6 copy-done.3
  145.4 2.1 fusion.55
  147.6 0.6 copy-done.7
  149.0 67.0 %reduce-scatter.3.cloned.1.call-done = f32[16,4096]{1,0:T(8,128)} async-done(((f32[128,4096]{1,0:T(8,128)}), f32[16,4096]{1,0:T(8,128)}) %reduce-scatter.3.cloned.1.call-update) | async-done | bytes 262160 | tf_op jit(solution)/shard_map/reduce_scatter | solution.py:160
  216.0 1.1 convert_reduce_fusion.2
  217.9 0.5 broadcast_in_dim.38
  218.3 0.5 dynamic-slice_bitcast_fusion
  218.9 0.6 collective-permute-start
  219.5 2.0 collective-permute-start.1
  221.4 1.1 collective-permute-start.2
  222.5 1.3 collective-permute-start.3
  223.8 1.6 collective-permute-start.4
  225.4 2.1 collective-permute-start.5
  227.6 2.8 collective-permute-start.6
  230.5 0.4 collective-permute-done.2
  230.9 8.9 %collective-permute-done.3 = bf16[4,4,4096]{2,1,0:T(4,128)(2,1)S(1)} collective-permute-done((bf16[4,4,4096]{2,1,0:T(4,128)(2,1)S(1)}, bf16[4,4,4096]{2,1,0:T(4,128)(2,1)S(1)}, u32[]{:S(2)}, u32[]{:S(2)}) %collective-permute-start.3) | collective-permute-done | bytes 131104 | tf_op jit(solution)/shard_map/ppermute | solution.py:183
  239.9 2.8 collective-permute-done.4
  243.0 1.4 gather_fusion
  244.4 1.6 copy.64
  246.2 36.3 %all-gather.6.cloned.1.call-done = bf16[32,4,4,4096]{3,0,2,1:T(8,128)(2,1)} async-done(((bf16[8,4,4,4096]{3,0,2,1:T(8,128)(2,1)}), bf16[32,4,4,4096]{3,0,2,1:T(8,128)(2,1)}) %all-gather.6.cloned.1.call-update) | async-done | bytes 4194320 | tf_op jit(solution)/shard_map/all_gather | solution.py:188
  282.5 16.1 %fusion.4 = f32[4,32,4,800]{3,1,2,0:T(8,128)} fusion(bf16[32,4,4,4096]{3,0,2,1:T(8,128)(2,1)} %all-gather.6.cloned.1.call-done, bf16[4,4096,800]{1,2,0:T(8,128)(2,1)} %param.25), kind=kOutput, calls=%fused_computation.7 | convolution fusion | flops 3355443200 | bytes 32047104 | tf_op jit(solution)/shard_map/gscd,sdf->gscf/dot_general | solution.py:67
  298.6 15.3 %fusion.15 = bf16[32,4,4,800]{3,0,2,1:T(8,128)(2,1)S(1)} fusion(f32[4,32,4,800]{3,1,2,0:T(8,128)} %fusion.4, bf16[32,4,4,4096]{3,0,2,1:T(8,128)(2,1)} %all-gather.6.cloned.1.call-done, bf16[4,4096,800]{1,2,0:T(8,128)(2,1)} %param.26), kind=kOutput, calls=%fused_computation.24 | convolution fusion | flops 3357900800 | bytes 32866304 | tf_op jit(solution)/shard_map/gscd,sdf->gscf/dot_general | solution.py:68
  313.9 16.2 %fusion.6 = f32[32,4,4,4096]{3,0,2,1:T(8,128)} fusion(bf16[32,4,4,800]{3,0,2,1:T(8,128)(2,1)S(1)} %fusion.15, bf16[4,800,4096]{2,1,0:T(8,128)(2,1)} %param.27), kind=kOutput, calls=%fused_computation.9 | convolution fusion | flops 3355443200 | bytes 35422208 | tf_op jit(solution)/shard_map/gscf,sfd->gscd/dot_general | solution.py:70
  330.1 71.5 %reduce-scatter.5.cloned.1.call-done = f32[8,4,4,4096]{3,0,2,1:T(8,128)} async-done(((f32[32,4,4,4096]{3,0,2,1:T(8,128)}), f32[8,4,4,4096]{3,0,2,1:T(8,128)}) %reduce-scatter.5.cloned.1.call-update) | async-done | bytes 2097168 | tf_op jit(solution)/shard_map/reduce_scatter | solution.py:190
  401.7 1.7 convert_element_type.112
  403.4 1.8 copy.65
  405.2 5.5 %all-to-all-start = ((bf16[8,4,4,4096]{3,2,1,0:T(4,128)(2,1)}), bf16[8,4,4,4096]{3,2,1,0:T(4,128)(2,1)S(1)}, u32[]{:S(2)}, u32[]{:S(2)}) async-start(bf16[8,4,4,4096]{3,2,1,0:T(4,128)(2,1)} %copy.65), calls=%async_computation.2 | async-start | bytes 2097152 | tf_op jit(solution)/shard_map/all_to_all | solution.py:193
  411.5 0.7 gather_fusion.2
  412.5 23.9 %all-to-all-done = bf16[8,4,4,4096]{3,2,1,0:T(4,128)(2,1)S(1)} async-done(((bf16[8,4,4,4096]{3,2,1,0:T(4,128)(2,1)}), bf16[8,4,4,4096]{3,2,1,0:T(4,128)(2,1)S(1)}, u32[]{:S(2)}, u32[]{:S(2)}) %all-to-all-start) | async-done | bytes 1048608 | tf_op jit(solution)/shard_map/all_to_all | solution.py:193
  436.4 0.6 convert_reduce_fusion.1
  437.4 0.7 gather_fusion.1
  438.4 0.8 multiply_reduce_fusion
  439.3 10.7 %all_to_all.28 = bf16[16,8,512]{2,0,1:T(8,128)(2,1)S(1)} all-to-all(bf16[16,8,512]{2,0,1:T(8,128)(2,1)S(1)} %bitcast.137), channel_id=1, replica_groups=mesh['wide'=8,'narrow'=4] {'wide'}, dimensions={1} | all-to-all | bytes 262144 | tf_op jit(solution)/shard_map/all_to_all | solution.py:201
  450.0 0.7 copy.99
  (79 shorter events, 5.3 us)
Async XLA Ops:
  6.5 51.6 %copy-start = (bf16[512,1024]{1,0:T(8,128)(2,1)S(1)}, bf16[512,1024]{1,0:T(8,128)(2,1)}, u32[]{:S(2)}) copy-start(bf16[512,1024]{1,0:T(8,128)(2,1)} %param.17) | copy-start | bytes 3145732
  6.5 48.2 %copy-start.5 = (f32[4096]{0:T(1024)S(1)}, f32[4096]{0:T(1024)}, u32[]{:S(2)}) copy-start(f32[4096]{0:T(1024)} %param.15) | copy-start | bytes 49156
  6.5 45.0 %all-gather.4.cloned.1.call-start = ((), (), s32[]{:S(2)}) async-start(), calls=%async_computation.4 | async-start | bytes 1179648 | tf_op jit(solution)/shard_map/all_gather | solution.py:114
  7.3 208.7 %reduce-scatter.3.cloned.1.call-start = ((), (), s32[]{:S(2)}) async-start(), calls=%async_computation.5 | async-start | bytes 2359296 | tf_op jit(solution)/shard_map/reduce_scatter | solution.py:160
  51.5 3.2 copy-start.2
  58.1 1.2 copy-start.4
  143.2 2.2 copy-start.3
  147.5 0.7 copy-start.7
  147.5 69.8 %copy-start.6 = (f32[4096]{0:T(1024)S(1)}, f32[4096]{0:T(1024)}, u32[]{:S(2)}) copy-start(f32[4096]{0:T(1024)} %param.22) | copy-start | bytes 49156
  147.5 135.0 %all-gather.6.cloned.1.call-start = ((), (), s32[]{:S(2)}) async-start(), calls=%async_computation.7 | async-start | bytes 5242880 | tf_op jit(solution)/shard_map/all_gather | solution.py:188
  218.9 6.5 %collective-permute-start = (bf16[4,4,4096]{2,1,0:T(4,128)(2,1)S(1)}, bf16[4,4,4096]{2,1,0:T(4,128)(2,1)S(1)}, u32[]{:S(2)}, u32[]{:S(2)}) collective-permute-start(bf16[4,4,4096]{2,1,0:T(4,128)(2,1)S(1)} %get-tuple-element.21), channel_id=1, source_target_pairs={{0,4},{4,0},{8,12},{12,8},{16,20},{20,16},{24,28},{28,24},{1,5},{5... | collective-permute-start | bytes 393224 | tf_op jit(solution)/shard_map/ppermute | solution.py:183
  219.5 8.1 %collective-permute-start.1 = (bf16[4,4,4096]{2,1,0:T(4,128)(2,1)S(1)}, bf16[4,4,4096]{2,1,0:T(4,128)(2,1)S(1)}, u32[]{:S(2)}, u32[]{:S(2)}) collective-permute-start(bf16[4,4,4096]{2,1,0:T(4,128)(2,1)S(1)} %get-tuple-element.20), channel_id=1, source_target_pairs={{0,8},{4,12},{8,0},{12,4},{16,24},{20,28},{24,16},{28,20},{1,9},{5... | collective-permute-start | bytes 393224 | tf_op jit(solution)/shard_map/ppermute | solution.py:183
  221.4 9.4 %collective-permute-start.2 = (bf16[4,4,4096]{2,1,0:T(4,128)(2,1)S(1)}, bf16[4,4,4096]{2,1,0:T(4,128)(2,1)S(1)}, u32[]{:S(2)}, u32[]{:S(2)}) collective-permute-start(bf16[4,4,4096]{2,1,0:T(4,128)(2,1)S(1)} %get-tuple-element.19), channel_id=1, source_target_pairs={{0,12},{4,8},{8,4},{12,0},{16,28},{20,24},{24,20},{28,16},{1,13},{... | collective-permute-start | bytes 393224 | tf_op jit(solution)/shard_map/ppermute | solution.py:183
  222.5 17.4 %collective-permute-start.3 = (bf16[4,4,4096]{2,1,0:T(4,128)(2,1)S(1)}, bf16[4,4,4096]{2,1,0:T(4,128)(2,1)S(1)}, u32[]{:S(2)}, u32[]{:S(2)}) collective-permute-start(bf16[4,4,4096]{2,1,0:T(4,128)(2,1)S(1)} %get-tuple-element.18), channel_id=1, source_target_pairs={{0,16},{4,20},{8,24},{12,28},{16,0},{20,4},{24,8},{28,12},{1,17},{... | collective-permute-start | bytes 393224 | tf_op jit(solution)/shard_map/ppermute | solution.py:183
  223.8 19.0 %collective-permute-start.4 = (bf16[4,4,4096]{2,1,0:T(4,128)(2,1)S(1)}, bf16[4,4,4096]{2,1,0:T(4,128)(2,1)S(1)}, u32[]{:S(2)}, u32[]{:S(2)}) collective-permute-start(bf16[4,4,4096]{2,1,0:T(4,128)(2,1)S(1)} %get-tuple-element.17), channel_id=1, source_target_pairs={{0,20},{4,16},{8,28},{12,24},{16,4},{20,0},{24,12},{28,8},{1,21},{... | collective-permute-start | bytes 393224 | tf_op jit(solution)/shard_map/ppermute | solution.py:183
  225.4 17.4 %collective-permute-start.5 = (bf16[4,4,4096]{2,1,0:T(4,128)(2,1)S(1)}, bf16[4,4,4096]{2,1,0:T(4,128)(2,1)S(1)}, u32[]{:S(2)}, u32[]{:S(2)}) collective-permute-start(bf16[4,4,4096]{2,1,0:T(4,128)(2,1)S(1)} %get-tuple-element.16), channel_id=1, source_target_pairs={{0,24},{4,28},{8,16},{12,20},{16,8},{20,12},{24,0},{28,4},{1,25},{... | collective-permute-start | bytes 393224 | tf_op jit(solution)/shard_map/ppermute | solution.py:183
  227.6 15.3 %collective-permute-start.6 = (bf16[4,4,4096]{2,1,0:T(4,128)(2,1)S(1)}, bf16[4,4,4096]{2,1,0:T(4,128)(2,1)S(1)}, u32[]{:S(2)}, u32[]{:S(2)}) collective-permute-start(bf16[4,4,4096]{2,1,0:T(4,128)(2,1)S(1)} %get-tuple-element.15), channel_id=1, source_target_pairs={{0,28},{4,24},{8,20},{12,16},{16,12},{20,8},{24,4},{28,0},{1,29},{... | collective-permute-start | bytes 393224 | tf_op jit(solution)/shard_map/ppermute | solution.py:183
  246.0 155.7 %reduce-scatter.5.cloned.1.call-start = ((), (), s32[]{:S(2)}) async-start(), calls=%async_computation.6 | async-start | bytes 10485760 | tf_op jit(solution)/shard_map/reduce_scatter | solution.py:190
  403.4 7.8 %copy-start.8 = (bf16[4096,16]{0,1:T(8,128)(2,1)S(1)}, bf16[4096,16]{0,1:T(8,128)(2,1)}, u32[]{:S(2)}) copy-start(bf16[4096,16]{0,1:T(8,128)(2,1)} %param.23) | copy-start | bytes 393220
  405.2 31.2 %all-to-all-start = ((bf16[8,4,4,4096]{3,2,1,0:T(4,128)(2,1)}), bf16[8,4,4,4096]{3,2,1,0:T(4,128)(2,1)S(1)}, u32[]{:S(2)}, u32[]{:S(2)}) async-start(bf16[8,4,4,4096]{3,2,1,0:T(4,128)(2,1)} %copy.65), calls=%async_computation.2 | async-start | bytes 2097152 | tf_op jit(solution)/shard_map/all_to_all | solution.py:193
  437.4 13.2 %copy-start.1 = (bf16[512,1024]{1,0:T(8,128)(2,1)S(1)}, bf16[512,1024]{1,0:T(8,128)(2,1)}, u32[]{:S(2)}) copy-start(bf16[512,1024]{1,0:T(8,128)(2,1)} %param.17) | copy-start | bytes 3145732
Sparse Core Ops, SparseCore 0:
  9.4 42.1 all-gather.3
  147.6 68.2 reduce-scatter.2
  246.1 36.3 all-gather.5
  330.2 71.3 reduce-scatter.4
